TPU v7x, 128 devices: a whole 4x4x4 slice. The times are simulated.
128 devices in a mesh: section: 2 (over core), seq: 4 (over z), shard: 16 (over x, y).
Axes of the slice: x: 4, y: 4, z: 4, core: 2. Of those that a mesh axis runs over, the one named last changes fastest.
Arguments:
- ends: bfloat16 [2, 16, 4, 256, 768], P('section', 'shard', None, 'seq'), may hold values from -6 to 6
- w_qkv: bfloat16 [2, 768, 2304], P('section', ('seq', 'shard')), may hold values from -0.21875 to 0.21875
- w_out: bfloat16 [2, 768, 768], P('section', ('seq', 'shard')), may hold values from -1.25 to 1.25
- w_up: bfloat16 [2, 768, 3072], P('section', ('seq', 'shard')), may hold values from -0.21875 to 0.21875
- w_down: bfloat16 [2, 3072, 768], P('section', ('seq', 'shard')), may hold values from -0.109375 to 0.109375
- norm_gains: bfloat16 [2, 2, 768], P('section', None, ('seq', 'shard')), may hold values from 0.25 to 1.75
- biases: bfloat16 [2, 6, 768], P('section', None, ('seq', 'shard')), may hold values from -3 to 3
- up_bias: bfloat16 [2, 3072], P('section', ('seq', 'shard')), may hold values from -3 to 3
Outputs:
- boundary: bfloat16 [2, 16, 4, 256, 768], P('section', 'shard', None, 'seq')
- grad_qkv: float32 [2, 768, 2304], P('section', ('seq', 'shard'))
- grad_out: float32 [2, 768, 768], P('section', ('seq', 'shard'))
- grad_up: float32 [2, 768, 3072], P('section', ('seq', 'shard'))
- grad_down: float32 [2, 3072, 768], P('section', ('seq', 'shard'))
- grad_gains: float32 [2, 2, 768], P('section', None, ('seq', 'shard'))
- grad_biases: float32 [2, 6, 768], P('section', None, ('seq', 'shard'))
- grad_up_bias: float32 [2, 3072], P('section', ('seq', 'shard'))
All inputs are finite; a program needn't handle non-finite values.
Results may differ from a plain program's by a relative error of at most 0.015.
Values may be sent and summed in bfloat16 or wider, within the bound.
A program may use at most 320 MiB of HBM per device.

v0:
```python
import jax
import jax.numpy as jnp
from jax import lax
from jax.sharding import PartitionSpec as P

HEAD = 64
FF = 3072
GROUP = 256
GROUPS = 4


EPSILON = 1e-05
MASKED = -1e30


def from_behind(x, axis, by):
    length = lax.axis_size(axis)
    pairs = [(i, i + by) for i in range(length) if 0 <= i + by < length]
    return lax.ppermute(x, axis, pairs)


def layer_norm(values, gain, shift):
    centre = jnp.mean(values, axis=-1, keepdims=True)
    centered = values - centre
    spread = jnp.mean(centered * centered, axis=-1, keepdims=True)
    return centered * lax.rsqrt(spread + EPSILON) * gain + shift


def gelu_tanh(values):
    return jax.nn.gelu(values, approximate=True)


def gather_weights(
    shard_qkv, shard_out, shard_up, shard_down, shard_gains, shard_shifts, shard_upbias
):
    whole = (
        lax.all_gather(shard_qkv, ("seq", "shard"), axis=1, tiled=True),
        lax.all_gather(shard_out, ("seq", "shard"), axis=1, tiled=True),
        lax.all_gather(shard_up, ("seq", "shard"), axis=1, tiled=True),
        lax.all_gather(shard_down, ("seq", "shard"), axis=1, tiled=True),
        lax.all_gather(shard_gains, ("seq", "shard"), axis=2, tiled=True),
        lax.all_gather(shard_shifts, ("seq", "shard"), axis=2, tiled=True),
        lax.all_gather(shard_upbias, ("seq", "shard"), axis=1, tiled=True),
    )
    return (
        whole[0][0],
        whole[1][0],
        whole[2][0],
        whole[3][0],
        whole[4][0].astype(jnp.float32),
        whole[5][0].astype(jnp.float32),
        whole[6][0].astype(jnp.float32),
    )


def reduce_grads(g_qkv, g_out, g_up, g_down, g_gains, g_shifts, g_upbias):
    return (
        lax.psum_scatter(g_qkv, ("seq", "shard"), scatter_dimension=0, tiled=True),
        lax.psum_scatter(g_out, ("seq", "shard"), scatter_dimension=0, tiled=True),
        lax.psum_scatter(g_up, ("seq", "shard"), scatter_dimension=0, tiled=True),
        lax.psum_scatter(g_down, ("seq", "shard"), scatter_dimension=0, tiled=True),
        lax.psum_scatter(g_gains, ("seq", "shard"), scatter_dimension=1, tiled=True),
        lax.psum_scatter(g_shifts, ("seq", "shard"), scatter_dimension=1, tiled=True),
        lax.psum_scatter(g_upbias, ("seq", "shard"), scatter_dimension=0, tiled=True),
    )


def store_group(buffer, new_entry, group_slot, is_live):
    updated = lax.dynamic_update_index_in_dim(buffer, new_entry, group_slot, 0)
    return jnp.where(is_live, updated, buffer)


def masked_scores(queries, key_heads, first_row, scaling):
    product = jnp.einsum("qhd,khd->hqk", queries, key_heads, preferred_element_type=jnp.float32)
    row_count = queries.shape[0]
    length = key_heads.shape[0]
    row_pos = first_row + lax.broadcasted_iota(jnp.int32, (row_count, length), 0)
    col_pos = lax.broadcasted_iota(jnp.int32, (row_count, length), 1)
    return jnp.where((col_pos <= row_pos)[None], product * scaling, MASKED)


def blocked_rows(queries, first_row):
    total_rows = queries.shape[0]
    block_rows = min(total_rows, 512)
    block_count = total_rows // block_rows
    blocked = queries.reshape(block_count, block_rows, queries.shape[1], queries.shape[2])
    starts = first_row + jnp.arange(block_count, dtype=jnp.int32) * block_rows
    return (blocked, starts)


def attend(queries, key_heads, value_heads, first_row):
    scaling = queries.shape[-1] ** (-0.5)
    blocked, starts = blocked_rows(queries, first_row)

    def one_block(packed):
        block_queries, block_first = packed
        scores = masked_scores(block_queries, key_heads, block_first, scaling)
        highest = jnp.max(scores, axis=-1, keepdims=True)
        exponent = jnp.exp(scores - highest)
        totals = jnp.sum(exponent, axis=-1, keepdims=True)
        chances = (exponent / totals).astype(jnp.bfloat16)
        mixed = jnp.einsum("hqk,khd->qhd", chances, value_heads, preferred_element_type=jnp.float32)
        return (mixed.astype(jnp.bfloat16), (highest + jnp.log(totals))[..., 0])

    outputs, log_sums = lax.map(one_block, (blocked, starts))
    return (outputs.reshape(queries.shape), log_sums)


def attend_back(queries, key_heads, value_heads, log_sums, grad_heads, first_row):
    scaling = queries.shape[-1] ** (-0.5)
    blocked, starts = blocked_rows(queries, first_row)
    blocked_grad = grad_heads.reshape(blocked.shape)

    def one_block(carry, packed):
        block_queries, block_grad, block_lse, block_first = packed
        scores = masked_scores(block_queries, key_heads, block_first, scaling)
        chances = jnp.exp(scores - block_lse[..., None])
        grad_chances = jnp.einsum(
            "qhd,khd->hqk", block_grad, value_heads, preferred_element_type=jnp.float32
        )
        centre = jnp.sum(chances * grad_chances, axis=-1, keepdims=True)
        grad_scores = (chances * (grad_chances - centre)).astype(jnp.bfloat16)
        grad_query = (
            jnp.einsum("hqk,khd->qhd", grad_scores, key_heads, preferred_element_type=jnp.float32)
            * scaling
        )
        grad_key = (
            carry[0]
            + jnp.einsum(
                "hqk,qhd->khd", grad_scores, block_queries, preferred_element_type=jnp.float32
            )
            * scaling
        )
        grad_value = carry[1] + jnp.einsum(
            "hqk,qhd->khd",
            chances.astype(jnp.bfloat16),
            block_grad,
            preferred_element_type=jnp.float32,
        )
        return ((grad_key, grad_value), grad_query)

    zeros = jnp.zeros(key_heads.shape, jnp.float32)
    (grad_keys, grad_values), grad_queries = lax.scan(
        one_block, (zeros, zeros), (blocked, blocked_grad, log_sums, starts)
    )
    return (grad_queries.reshape(queries.shape), grad_keys, grad_values)


def forward_group(hidden, group_index, is_live, weights, kv_store, key_limit):
    w_qkv, w_out, w_up, w_down, gains, shifts, up_bias = weights
    parts = lax.axis_size("seq")
    local_rows, width = hidden.shape
    normed = layer_norm(hidden, gains[0], shifts[0]).astype(jnp.bfloat16)
    qkv_bias = jnp.concatenate([shifts[2], jnp.zeros_like(shifts[2]), shifts[3]])
    projected = (jnp.dot(normed, w_qkv, preferred_element_type=jnp.float32) + qkv_bias).astype(
        jnp.bfloat16
    )
    by_heads = lax.all_to_all(
        projected.reshape(local_rows, 3, parts, width // parts),
        "seq",
        split_axis=2,
        concat_axis=0,
        tiled=True,
    )
    group_rows = by_heads.shape[0]
    head_count = width // parts // HEAD
    split = by_heads.reshape(group_rows, 3, head_count, HEAD)
    queries = split[:, 0]
    fresh = jnp.stack([split[:, 1], split[:, 2]])
    first_row = jnp.clip(group_index, 0, GROUPS - 1) * group_rows
    updated = lax.dynamic_update_slice_in_dim(kv_store, fresh, first_row, 1)
    kv_store = jnp.where(is_live, updated, kv_store)
    visible = kv_store[:, :key_limit]
    mixed_heads, log_sums = attend(queries, visible[0], visible[1], first_row)
    returned = lax.all_to_all(
        mixed_heads.reshape(group_rows, 1, width // parts),
        "seq",
        split_axis=0,
        concat_axis=1,
        tiled=True,
    )
    mixed = returned.reshape(local_rows, width)
    middle = hidden + (jnp.dot(mixed, w_out, preferred_element_type=jnp.float32) + shifts[4])
    normed_two = layer_norm(middle, gains[1], shifts[1]).astype(jnp.bfloat16)
    raised = jnp.dot(normed_two, w_up, preferred_element_type=jnp.float32) + up_bias
    active = gelu_tanh(raised).astype(jnp.bfloat16)
    result = middle + (jnp.dot(active, w_down, preferred_element_type=jnp.float32) + shifts[5])
    return (result, (queries, log_sums, mixed, middle, raised), kv_store)


def backward_group(
    grad_result, group_index, is_live, weights, kv_store, kv_grads, hidden, saved, key_limit
):
    w_qkv, w_out, w_up, w_down, gains, shifts, up_bias = weights
    queries, log_sums, mixed, middle, raised = saved
    parts = lax.axis_size("seq")
    local_rows, width = hidden.shape
    grad_low = grad_result.astype(jnp.bfloat16)
    active = gelu_tanh(raised).astype(jnp.bfloat16)
    g_down = jnp.dot(active.T, grad_low, preferred_element_type=jnp.float32)
    grad_active = jnp.dot(grad_low, w_down.T, preferred_element_type=jnp.float32)
    unused_gelu, gelu_pull = jax.vjp(gelu_tanh, raised)
    grad_raised = gelu_pull(grad_active)[0].astype(jnp.bfloat16)
    normed_two, second_pull = jax.vjp(layer_norm, middle, gains[1], shifts[1])
    g_up = jnp.dot(
        normed_two.astype(jnp.bfloat16).T, grad_raised, preferred_element_type=jnp.float32
    )
    grad_normed_two = jnp.dot(grad_raised, w_up.T, preferred_element_type=jnp.float32)
    grad_middle, grad_gain_two, grad_shift_two = second_pull(grad_normed_two)
    grad_middle = grad_middle + grad_result
    grad_branch = grad_middle.astype(jnp.bfloat16)
    g_out = jnp.dot(mixed.T, grad_branch, preferred_element_type=jnp.float32)
    grad_mixed = jnp.dot(grad_branch, w_out.T, preferred_element_type=jnp.float32).astype(
        jnp.bfloat16
    )
    heads_grad = lax.all_to_all(
        grad_mixed.reshape(local_rows, parts, width // parts),
        "seq",
        split_axis=1,
        concat_axis=0,
        tiled=True,
    )
    group_rows = heads_grad.shape[0]
    heads_grad = heads_grad.reshape(queries.shape)
    first_row = jnp.clip(group_index, 0, GROUPS - 1) * group_rows
    visible = kv_store[:, :key_limit]
    grad_queries, grad_keys, grad_values = attend_back(
        queries, visible[0], visible[1], log_sums, heads_grad, first_row
    )
    addition = jnp.where(is_live, jnp.stack([grad_keys, grad_values]), 0.0)
    kv_grads = kv_grads.at[:, :key_limit].add(addition)
    own_grads = lax.dynamic_slice_in_dim(kv_grads, first_row, group_rows, 1)
    grad_split = jnp.stack([grad_queries, own_grads[0], own_grads[1]], axis=1).astype(jnp.bfloat16)
    tokens_grad = lax.all_to_all(
        grad_split.reshape(group_rows, 3, 1, width // parts),
        "seq",
        split_axis=0,
        concat_axis=2,
        tiled=True,
    )
    grad_projected = tokens_grad.reshape(local_rows, 3 * width)
    normed, first_pull = jax.vjp(layer_norm, hidden, gains[0], shifts[0])
    g_qkv = jnp.dot(
        normed.astype(jnp.bfloat16).T, grad_projected, preferred_element_type=jnp.float32
    )
    grad_normed = jnp.dot(grad_projected, w_qkv.T, preferred_element_type=jnp.float32)
    grad_hidden, grad_gain_one, grad_shift_one = first_pull(grad_normed)
    grad_hidden = grad_hidden + grad_middle
    column_sums = jnp.sum(grad_projected.astype(jnp.float32), axis=0).reshape(3, width)
    g_gains = jnp.stack([grad_gain_one, grad_gain_two])
    g_shifts = jnp.stack(
        [
            grad_shift_one,
            grad_shift_two,
            column_sums[0],
            column_sums[2],
            jnp.sum(grad_branch.astype(jnp.float32), axis=0),
            jnp.sum(grad_low.astype(jnp.float32), axis=0),
        ]
    )
    g_upbias = jnp.sum(grad_raised.astype(jnp.float32), axis=0)
    grads = (g_qkv, g_out, g_up, g_down, g_gains, g_shifts, g_upbias)
    grads = tuple((jnp.where(is_live, item, 0.0) for item in grads))
    return (grad_hidden, grads, kv_grads)


def per_device(ends, w_qkv, w_out, w_up, w_down, norm_gains, biases, up_bias):
    section_index = lax.axis_index("section")
    section_count = lax.axis_size("section")
    own_data = ends[0, 0]
    local_rows = own_data.shape[1]
    width = own_data.shape[2]
    parts = lax.axis_size("seq")
    head_count = width // parts // HEAD
    seq_length = GROUPS * GROUP
    block_rows = min(GROUP, 512)
    weights = gather_weights(w_qkv, w_out, w_up, w_down, norm_gains, biases, up_bias)
    kv_store = jnp.zeros((2, seq_length, head_count, HEAD), jnp.bfloat16)
    hidden_store = jnp.zeros_like(own_data)
    stores = (
        jnp.zeros((GROUPS, GROUP, head_count, HEAD), jnp.bfloat16),
        jnp.zeros((GROUPS, GROUP // block_rows, head_count, block_rows), jnp.float32),
        jnp.zeros((GROUPS, local_rows, width), jnp.bfloat16),
        jnp.zeros((GROUPS, local_rows, width), jnp.float32),
        jnp.zeros((GROUPS, local_rows, FF), jnp.float32),
    )
    result_store = jnp.zeros_like(own_data)
    tick_count = GROUPS + section_count - 1
    arriving = jnp.zeros((local_rows, width), jnp.bfloat16)
    for tick_index in range(tick_count):
        group_index = tick_index - section_index
        is_live = (group_index >= 0) & (group_index < GROUPS)
        group_slot = jnp.clip(group_index, 0, GROUPS - 1)
        key_limit = min(tick_index + 1, GROUPS) * GROUP
        own_block = lax.dynamic_index_in_dim(own_data, group_slot, 0, keepdims=False)
        entering = jnp.where(section_index == 0, own_block, arriving)
        result, saved, kv_store = forward_group(
            entering.astype(jnp.float32), group_index, is_live, weights, kv_store, key_limit
        )
        hidden_store = store_group(hidden_store, entering, group_slot, is_live)
        stores = tuple(
            (store_group(buffer, item, group_slot, is_live) for buffer, item in zip(stores, saved))
        )
        outgoing = result.astype(jnp.bfloat16)
        result_store = store_group(result_store, outgoing, group_slot, is_live)
        if tick_index + 1 < tick_count:
            arriving = from_behind(outgoing, "section", 1)
    kv_grads = jnp.zeros((2, seq_length, head_count, HEAD), jnp.float32)
    input_store = jnp.zeros_like(own_data)
    arriving = jnp.zeros((local_rows, width), jnp.bfloat16)
    totals = None
    for tick_index in range(tick_count):
        group_index = GROUPS - 1 - tick_index + (section_count - 1 - section_index)
        is_live = (group_index >= 0) & (group_index < GROUPS)
        group_slot = jnp.clip(group_index, 0, GROUPS - 1)
        key_limit = max(min(GROUPS + 1 - tick_index, GROUPS), 1) * GROUP
        own_block = lax.dynamic_index_in_dim(own_data, group_slot, 0, keepdims=False)
        entering = jnp.where(section_index == section_count - 1, own_block, arriving).astype(
            jnp.float32
        )
        saved = tuple(
            (lax.dynamic_index_in_dim(buffer, group_slot, 0, keepdims=False) for buffer in stores)
        )
        hidden = lax.dynamic_index_in_dim(hidden_store, group_slot, 0, keepdims=False).astype(
            jnp.float32
        )
        grad_hidden, grads, kv_grads = backward_group(
            entering, group_index, is_live, weights, kv_store, kv_grads, hidden, saved, key_limit
        )
        outgoing = grad_hidden.astype(jnp.bfloat16)
        input_store = store_group(input_store, outgoing, group_slot, is_live)
        if tick_index + 1 < tick_count:
            arriving = from_behind(outgoing, "section", -1)
        if totals is None:
            totals = grads
        else:
            totals = tuple(
                (first_part + second_part for first_part, second_part in zip(totals, grads))
            )
    totals = reduce_grads(
        totals[0], totals[1], totals[2], totals[3], totals[4], totals[5], totals[6]
    )
    boundary = jnp.where(section_index == 0, input_store, result_store)[None, None]
    return (
        boundary,
        totals[0][None],
        totals[1][None],
        totals[2][None],
        totals[3][None],
        totals[4][None],
        totals[5][None],
        totals[6][None],
    )


def solution(mesh):
    placed = (
        P("section", "shard", None, "seq", None),
        P("section", ("seq", "shard"), None),
        P("section", ("seq", "shard"), None),
        P("section", ("seq", "shard"), None),
        P("section", ("seq", "shard"), None),
        P("section", None, ("seq", "shard")),
        P("section", None, ("seq", "shard")),
        P("section", ("seq", "shard")),
    )
    return jax.shard_map(
        per_device,
        mesh=mesh,
        in_specs=placed,
        out_specs=(
            P("section", "shard", None, "seq", None),
            P("section", ("seq", "shard"), None),
            P("section", ("seq", "shard"), None),
            P("section", ("seq", "shard"), None),
            P("section", ("seq", "shard"), None),
            P("section", None, ("seq", "shard")),
            P("section", None, ("seq", "shard")),
            P("section", ("seq", "shard")),
        ),
        check_vma=False,
    )
```

profile of v0, /device:TPU:2, one launch (start us, length us, event | category | flops | bytes accessed | tf_op | source)
XLA Modules:
  0.0 2362.7 jit_solution(1772695840109049700)
XLA Ops:
  20.2 172.8 %all-reduce = bf16[3072]{0:T(1024)(128)(2,1)S(1)} all-reduce(bf16[3072]{0:T(1024)(128)(2,1)S(1)} %dynamic-update-slice.58), channel_id=1, replica_groups=mesh['section'=2,'seq'=4,'shard'=16] {'seq','shard'}, use_global_device_ids=true, to_apply=%add | all-reduce | flops 3072 | bytes 12288
  193.6 172.2 %all_gather.22 = bf16[1,6,768]{1,0,2:T(2,128)(2,1)S(1)} all-gather(bf16[1,6,12]{1,0,2:T(2,128)(2,1)S(1)} %copy.210), channel_id=1, replica_groups=mesh['section'=2,'seq'=4,'shard'=16] {'seq','shard'}, dimensions={2}, use_global_device_ids=true | all-gather | bytes 9360 | tf_op jit(solution)/shard_map/all_gather | solution.py:42
  366.2 173.5 %all_gather.21 = bf16[1,2,768]{1,0,2:T(2,128)(2,1)S(1)} all-gather(bf16[1,2,12]{1,0,2:T(2,128)(2,1)S(1)} %copy.209), channel_id=1, replica_groups=mesh['section'=2,'seq'=4,'shard'=16] {'seq','shard'}, dimensions={2}, use_global_device_ids=true | all-gather | bytes 3120 | tf_op jit(solution)/shard_map/all_gather | solution.py:41
  541.4 13.9 slice_reduce_fusion
  624.0 5.4 copy.293
  656.8 5.8 all-to-all-done.2
  726.1 5.8 all-to-all-done.4
  796.5 5.8 all-to-all-done.6
  866.1 5.8 all-to-all-done.8
  924.9 6.3 fusion.392
  934.7 6.1 fusion.551
  994.8 7.0 all-to-all-done.11
  1009.6 5.2 fusion.567
  1029.4 6.3 fusion.375
  1035.7 4.9 convert_reduce_fusion.3
  1040.6 6.2 fusion.552
  1094.7 4.9 all-to-all-start.13
  1100.8 9.6 all-to-all-done.13
  1118.3 5.1 fusion.564
  1136.8 6.1 fusion.377
  1147.9 6.1 fusion.553
  1209.0 9.6 all-to-all-done.15
  1226.5 5.0 fusion.561
  1245.3 6.1 fusion.379
  1251.4 4.9 convert_reduce_fusion.1
  1256.3 6.1 fusion.554
  1316.3 9.2 all-to-all-done.17
  1333.4 5.0 fusion.558
  1364.4 15.1 select_add_fusion
  1391.7 16.3 select_add_fusion.1
  1408.1 5.0 select_add_fusion.3
  1442.2 7.4 all-to-all-done.19
  1459.2 11.8 select_add_fusion.2
  1471.1 290.3 %fusion.834 = (f32[16,2304]{1,0:T(8,128)}, f32[16,768]{1,0:T(8,128)S(1)}, f32[16,3072]{1,0:T(8,128)S(1)}) fusion(f32[768,2304]{1,0:T(8,128)} %select_add_fusion.2, f32[768,768]{1,0:T(8,128)S(1)} %copy-done.10, f32[768,3072]{1,0:T(8,128)} %select_add_fusion.1), kind=kCustom, calls=%all-reduce-scatter.3 | all-reduce-scatter fusion | flops 6291457 | bytes 19268096
  1765.2 6.9 collective-permute-start.37
  1784.8 9.5 collective-permute-start.33
  1800.0 6.0 collective-permute-start.30
  1829.7 333.4 %all-reduce.10 = (f32[2,768]{1,0:T(2,128)}, f32[6,768]{1,0:T(8,128)}, f32[3072]{0:T(1024)}) all-reduce(f32[2,768]{1,0:T(2,128)S(1)} %fusion.760, f32[6,768]{1,0:T(8,128)S(1)} %select_add_fusion.4, f32[3072]{0:T(1024)S(1)} %copy-done.112), channel_id=6, replica_groups=mesh['section'=2,'seq'=4,'shard'=16] {'seq','shard'}, use_global_device_ids=true, to_apply=%region_89.90.clone | all-reduce | flops 9216 | bytes 73728
  2169.7 20.4 collective-permute-start.16
  2191.5 7.9 collective-permute-start.14
  2208.5 6.5 collective-permute-start.10
  2226.9 5.5 collective-permute-start.54
  2250.3 12.0 collective-permute-start.47
  2262.3 5.9 collective-permute-start.46
  2268.2 5.0 collective-permute-start.45
  2274.4 11.0 concatenate.71
  2286.3 16.7 concatenate.70
  2325.1 30.0 %concatenate.72 = f32[268,3072]{1,0:T(8,128)S(1)} concatenate(f32[12,3072]{1,0:T(8,128)} %copy-done.74, f32[16,3072]{1,0:T(8,128)} %copy-done.75, f32[16,3072]{1,0:T(8,128)} %copy-done.76, f32[16,3072]{1,0:T(8,128)} %copy-done.77, f32[16,3072]{1,0:T(8,128)} %copy-done.78, f32[16,3072]{1,0:T(8,128)} %copy-done.79, f32[16,3072]{1,0:T(8,128)} %collective-permute-done.49, ...), dimensions={0} | concatenate | bytes 6586368
  (974 shorter events, 839.8 us)
Async XLA Ops:
  7.2 559.0 %all-gather.5.cloned.1.call-start = ((), (), s32[]{:S(2)}) async-start(), calls=%async_computation.21 | async-start | bytes 7188480 | tf_op jit(solution)/shard_map/all_gather | solution.py:37
  8.9 572.9 %all-gather.7.cloned.1.call-start = ((), (), s32[]{:S(2)}) async-start(), calls=%async_computation.22 | async-start | bytes 2396160 | tf_op jit(solution)/shard_map/all_gather | solution.py:38
  10.4 613.6 %all-gather.9.cloned.1.call-start = ((), (), s32[]{:S(2)}) async-start(), calls=%async_computation.23 | async-start | bytes 9584640 | tf_op jit(solution)/shard_map/all_gather | solution.py:39
  12.1 622.5 %all-gather.11.cloned.1.call-start = ((), (), s32[]{:S(2)}) async-start(), calls=%async_computation.24 | async-start | bytes 4792320 | tf_op jit(solution)/shard_map/all_gather | solution.py:40
  1094.7 15.7 all-to-all-start.13
  1203.1 15.6 all-to-all-start.15
  1309.9 15.6 all-to-all-start.17
  1314.7 1041.3 %reduce-scatter.10.cloned.1.call-start = ((), (), s32[]{:S(2)}) async-start(), calls=%async_computation.25 | async-start | bytes 9584640 | tf_op jit(solution)/shard_map/reduce_scatter | solution.py:61
  1387.6 27.8 %all-to-all-start.18 = ((bf16[64,4,192]{2,0,1:T(8,128)(2,1)}), bf16[64,4,192]{2,0,1:T(8,128)(2,1)}, u32[]{:S(2)}, u32[]{:S(2)}) async-start(bf16[64,4,192]{2,0,1:T(8,128)(2,1)} %copy.263), calls=%async_computation.18 | async-start | bytes 262144 | tf_op jit(solution)/shard_map/all_to_all | solution.py:216
  1761.3 23.4 collective-permute-start.38
  1765.2 29.1 %collective-permute-start.37 = (f32[16,768]{1,0:T(8,128)S(1)}, f32[16,768]{1,0:T(8,128)S(1)}, u32[]{:S(2)}, u32[]{:S(2)}) collective-permute-start(f32[16,768]{1,0:T(8,128)S(1)} %get-tuple-element.450), channel_id=1, source_target_pairs={{0,14},{1,15},{2,16},{3,17},{4,18},{5,19},{6,20},{7,21},{8,22},{9,... | collective-permute-start | bytes 147464
  1772.1 25.3 %collective-permute-start.36 = (f32[16,768]{1,0:T(8,128)S(1)}, f32[16,768]{1,0:T(8,128)S(1)}, u32[]{:S(2)}, u32[]{:S(2)}) collective-permute-start(f32[16,768]{1,0:T(8,128)S(1)} %get-tuple-element.450), channel_id=1, source_target_pairs={{0,13},{1,14},{2,15},{3,16},{4,17},{5,18},{6,19},{7,20},{8,21},{9,... | collective-permute-start | bytes 147464
  1776.0 23.9 %collective-permute-start.35 = (f32[16,768]{1,0:T(8,128)S(1)}, f32[16,768]{1,0:T(8,128)S(1)}, u32[]{:S(2)}, u32[]{:S(2)}) collective-permute-start(f32[16,768]{1,0:T(8,128)S(1)} %get-tuple-element.450), channel_id=1, source_target_pairs={{0,12},{1,13},{2,14},{3,15},{4,16},{5,17},{6,18},{7,19},{8,20},{9,... | collective-permute-start | bytes 147464
  1783.5 22.5 collective-permute-start.34
  1784.8 22.6 collective-permute-start.33
  1794.3 16.6 collective-permute-start.32
  1797.4 15.8 collective-permute-start.31
  1800.0 18.4 collective-permute-start.30
  1807.4 17.1 collective-permute-start.28
  1811.0 16.3 collective-permute-start.27
  1813.3 355.1 %collective-permute-start.22 = (f32[16,2304]{1,0:T(8,128)}, f32[16,2304]{1,0:T(8,128)S(1)}, u32[]{:S(2)}, u32[]{:S(2)}) collective-permute-start(f32[16,2304]{1,0:T(8,128)} %get-tuple-element.449), channel_id=1, source_target_pairs={{0,15},{1,16},{2,17},{3,18},{4,19},{5,20},{6,21},{7,22},{8,23},{9,... | collective-permute-start | bytes 442376
  1818.3 344.8 %collective-permute-start.26 = (f32[16,768]{1,0:T(8,128)S(1)}, f32[16,768]{1,0:T(8,128)}, u32[]{:S(2)}, u32[]{:S(2)}) collective-permute-start(f32[16,768]{1,0:T(8,128)S(1)} %get-tuple-element.450), channel_id=1, source_target_pairs={{0,3},{1,4},{2,5},{3,6},{4,7},{5,8},{6,9},{7,10},{8,11},{9,12},{10... | collective-permute-start | bytes 147464
  1821.1 343.3 %collective-permute-start.25 = (f32[16,768]{1,0:T(8,128)S(1)}, f32[16,768]{1,0:T(8,128)}, u32[]{:S(2)}, u32[]{:S(2)}) collective-permute-start(f32[16,768]{1,0:T(8,128)S(1)} %get-tuple-element.450), channel_id=1, source_target_pairs={{0,2},{1,3},{2,4},{3,5},{4,6},{5,7},{6,8},{7,9},{8,10},{9,11},{10,... | collective-permute-start | bytes 147464
  1824.5 341.2 %collective-permute-start.24 = (f32[16,768]{1,0:T(8,128)S(1)}, f32[16,768]{1,0:T(8,128)}, u32[]{:S(2)}, u32[]{:S(2)}) collective-permute-start(f32[16,768]{1,0:T(8,128)S(1)} %get-tuple-element.450), channel_id=1, source_target_pairs={{0,1},{1,2},{2,3},{3,4},{4,5},{5,6},{6,7},{7,8},{8,9},{9,10},{10,1... | collective-permute-start | bytes 147464
  1827.4 339.7 %collective-permute-start.23 = (f32[12,2304]{1,0:T(8,128)S(1)}, f32[12,2304]{1,0:T(8,128)S(1)}, u32[]{:S(2)}, u32[]{:S(2)}) collective-permute-start(f32[12,2304]{1,0:T(8,128)S(1)} %slice.582), channel_id=1, source_target_pairs={{0,16},{1,17},{2,18},{3,19},{4,20},{5,21},{6,22},{7,23},{8,24},{9,... | collective-permute-start | bytes 331784
  2164.4 25.7 %collective-permute-start.20 = (f32[16,2304]{1,0:T(8,128)}, f32[16,2304]{1,0:T(8,128)S(1)}, u32[]{:S(2)}, u32[]{:S(2)}) collective-permute-start(f32[16,2304]{1,0:T(8,128)} %get-tuple-element.449), channel_id=1, source_target_pairs={{0,13},{1,14},{2,15},{3,16},{4,17},{5,18},{6,19},{7,20},{8,21},{9,... | collective-permute-start | bytes 442376
  2165.7 25.7 %collective-permute-start.19 = (f32[16,2304]{1,0:T(8,128)}, f32[16,2304]{1,0:T(8,128)S(1)}, u32[]{:S(2)}, u32[]{:S(2)}) collective-permute-start(f32[16,2304]{1,0:T(8,128)} %get-tuple-element.449), channel_id=1, source_target_pairs={{0,12},{1,13},{2,14},{3,15},{4,16},{5,17},{6,18},{7,19},{8,20},{9,... | collective-permute-start | bytes 442376
  2167.1 32.4 %collective-permute-start.18 = (f32[16,2304]{1,0:T(8,128)}, f32[16,2304]{1,0:T(8,128)S(1)}, u32[]{:S(2)}, u32[]{:S(2)}) collective-permute-start(f32[16,2304]{1,0:T(8,128)} %get-tuple-element.449), channel_id=1, source_target_pairs={{0,11},{1,12},{2,13},{3,14},{4,15},{5,16},{6,17},{7,18},{8,19},{9,... | collective-permute-start | bytes 442376
  2168.4 32.4 %collective-permute-start.17 = (f32[16,2304]{1,0:T(8,128)}, f32[16,2304]{1,0:T(8,128)S(1)}, u32[]{:S(2)}, u32[]{:S(2)}) collective-permute-start(f32[16,2304]{1,0:T(8,128)} %get-tuple-element.449), channel_id=1, source_target_pairs={{0,10},{1,11},{2,12},{3,13},{4,14},{5,15},{6,16},{7,17},{8,18},{9,... | collective-permute-start | bytes 442376
  2169.7 36.5 %collective-permute-start.16 = (f32[16,2304]{1,0:T(8,128)}, f32[16,2304]{1,0:T(8,128)S(1)}, u32[]{:S(2)}, u32[]{:S(2)}) collective-permute-start(f32[16,2304]{1,0:T(8,128)} %get-tuple-element.449), channel_id=1, source_target_pairs={{0,9},{1,10},{2,11},{3,12},{4,13},{5,14},{6,15},{7,16},{8,17},{9,1... | collective-permute-start | bytes 442376
  2190.2 18.3 collective-permute-start.15
  2191.5 23.6 collective-permute-start.14
  2199.4 17.9 collective-permute-start.13
  2200.8 19.1 collective-permute-start.12
  2206.3 20.6 collective-permute-start.11
  2208.5 23.9 %collective-permute-start.10 = (f32[16,2304]{1,0:T(8,128)}, f32[16,2304]{1,0:T(8,128)}, u32[]{:S(2)}, u32[]{:S(2)}) collective-permute-start(f32[16,2304]{1,0:T(8,128)} %get-tuple-element.449), channel_id=1, source_target_pairs={{0,3},{1,4},{2,5},{3,6},{4,7},{5,8},{6,9},{7,10},{8,11},{9,12},{10... | collective-permute-start | bytes 442376
  2215.1 19.0 collective-permute-start.9
  2217.3 19.9 collective-permute-start.8
  2219.8 19.7 collective-permute-start.55
  2226.9 17.6 collective-permute-start.54
  2234.1 16.2 collective-permute-start.52
  2237.3 25.0 %collective-permute-start.51 = (f32[16,3072]{1,0:T(8,128)S(1)}, f32[16,3072]{1,0:T(8,128)S(1)}, u32[]{:S(2)}, u32[]{:S(2)}) collective-permute-start(f32[16,3072]{1,0:T(8,128)S(1)} %get-tuple-element.451), channel_id=1, source_target_pairs={{0,12},{1,13},{2,14},{3,15},{4,16},{5,17},{6,18},{7,19},{8,20},{9,... | collective-permute-start | bytes 589832
  2239.6 28.6 %collective-permute-start.50 = (f32[16,3072]{1,0:T(8,128)S(1)}, f32[16,3072]{1,0:T(8,128)S(1)}, u32[]{:S(2)}, u32[]{:S(2)}) collective-permute-start(f32[16,3072]{1,0:T(8,128)S(1)} %get-tuple-element.451), channel_id=1, source_target_pairs={{0,11},{1,12},{2,13},{3,14},{4,15},{5,16},{6,17},{7,18},{8,19},{9,... | collective-permute-start | bytes 589832
  2244.5 58.4 %collective-permute-start.49 = (f32[16,3072]{1,0:T(8,128)S(1)}, f32[16,3072]{1,0:T(8,128)}, u32[]{:S(2)}, u32[]{:S(2)}) collective-permute-start(f32[16,3072]{1,0:T(8,128)S(1)} %get-tuple-element.451), channel_id=1, source_target_pairs={{0,10},{1,11},{2,12},{3,13},{4,14},{5,15},{6,16},{7,17},{8,18},{9,... | collective-permute-start | bytes 589832
  2247.4 56.9 %collective-permute-start.48 = (f32[16,3072]{1,0:T(8,128)S(1)}, f32[16,3072]{1,0:T(8,128)}, u32[]{:S(2)}, u32[]{:S(2)}) collective-permute-start(f32[16,3072]{1,0:T(8,128)S(1)} %get-tuple-element.451), channel_id=1, source_target_pairs={{0,9},{1,10},{2,11},{3,12},{4,13},{5,14},{6,15},{7,16},{8,17},{9,1... | collective-permute-start | bytes 589832
  2250.3 57.4 %collective-permute-start.47 = (f32[16,3072]{1,0:T(8,128)S(1)}, f32[16,3072]{1,0:T(8,128)}, u32[]{:S(2)}, u32[]{:S(2)}) collective-permute-start(f32[16,3072]{1,0:T(8,128)S(1)} %get-tuple-element.451), channel_id=1, source_target_pairs={{0,8},{1,9},{2,10},{3,11},{4,12},{5,13},{6,14},{7,15},{8,16},{9,17... | collective-permute-start | bytes 589832
  2262.3 49.3 %collective-permute-start.46 = (f32[16,3072]{1,0:T(8,128)S(1)}, f32[16,3072]{1,0:T(8,128)}, u32[]{:S(2)}, u32[]{:S(2)}) collective-permute-start(f32[16,3072]{1,0:T(8,128)S(1)} %get-tuple-element.451), channel_id=1, source_target_pairs={{0,7},{1,8},{2,9},{3,10},{4,11},{5,12},{6,13},{7,14},{8,15},{9,16}... | collective-permute-start | bytes 589832
  2268.2 47.2 %collective-permute-start.45 = (f32[16,3072]{1,0:T(8,128)S(1)}, f32[16,3072]{1,0:T(8,128)}, u32[]{:S(2)}, u32[]{:S(2)}) collective-permute-start(f32[16,3072]{1,0:T(8,128)S(1)} %get-tuple-element.451), channel_id=1, source_target_pairs={{0,6},{1,7},{2,8},{3,9},{4,10},{5,11},{6,12},{7,13},{8,14},{9,15},... | collective-permute-start | bytes 589832
  (215 other events, 7903.8 us)
Sparse Core Ops, SparseCore 0:
  11.3 77.3 all-gather.4
  92.1 64.4 all-gather.6
  159.9 81.3 all-gather.8
  243.9 68.4 all-gather.10
  1379.7 448.9 reduce-scatter.9
where the time goes:
time: 2380 us; the launch traced here: 2360 us
  blocking collectives  1140 us (48%)
  local copies, waits for them, and re-layouts  364 us (15%)
  matrix products  311 us (13%)
  starting transfers between devices  279 us (12%)
  other arithmetic  152 us (6%)
  waiting for transfers between devices  96 us (4%)
    unnamed x3, blocking collectives  797 us
    unnamed x48, starting transfers between devices  180 us
    all_gather x1, blocking collectives, gather_weights(): lax.all_gather(shard_gains, ('seq', 'shard'), axis=2, tiled=True)  173 us
    all_gather x1, blocking collectives, gather_weights(): lax.all_gather(shard_shifts, ('seq', 'shard'), axis=2, tiled=True)  172 us
    unnamed x405, local copies, waits for them, and re-layouts  126 us
  transfers between devices with their start and end apart: 81, of which 17 were waited for; matrix products, arithmetic and copies ran while one was open for 26% of the time, Pallas kernels for 0%

commit v1 on v0

v1 whole, which is shorter than its diff:
```python
import functools

import jax
import jax.numpy as jnp
from jax import lax
from jax.experimental import pallas as pl
from jax.experimental.pallas import tpu as pltpu
from jax.sharding import PartitionSpec as P

HEAD = 64
FF = 3072
D = 768
GROUPS = 4
ROWS = 64
TOK = GROUPS * ROWS
SEQ_LEN = 1024
HL = 192
EPSILON = 1e-05
MASKED = -1e30
BF = jnp.bfloat16
F32 = jnp.float32
MESH = pl.DeviceIdType.MESH
HBM = pltpu.HBM


def sds(shape, dtype):
    return jax.ShapeDtypeStruct(shape, dtype)


def coords():
    shard = lax.axis_index("shard")
    return {"x": shard // 4, "y": lax.rem(shard, 4), "z": lax.axis_index("seq")}


def peer(c, axis, by):
    moved = dict(c)
    moved[axis] = lax.rem(c[axis] + by, 4)
    return {"section": lax.axis_index("section"), "seq": moved["z"], "shard": moved["x"] * 4 + moved["y"]}


def meet(c, axes, steps):
    barrier = pltpu.get_barrier_semaphore()
    for axis in axes:
        for by in steps:
            pl.semaphore_signal(barrier, inc=1, device_id=peer(c, axis, by), device_id_type=MESH)
    pl.semaphore_wait(barrier, len(axes) * len(steps))


class Copies:
    def __init__(self, send, recv):
        self.send, self.recv, self.used, self.sent = send, recv, 0, []

    def remote(self, src, dst, to):
        copy = pltpu.make_async_remote_copy(
            src_ref=src,
            dst_ref=dst,
            send_sem=self.send.at[self.used],
            recv_sem=self.recv.at[self.used],
            device_id=to,
            device_id_type=MESH,
        )
        self.used += 1
        copy.start()
        self.sent.append(copy)
        return copy

    def local(self, src, dst):
        copy = pltpu.make_async_copy(src, dst, self.send.at[self.used])
        self.used += 1
        copy.start()
        return copy

    def drain(self):
        for copy in self.sent:
            copy.wait_send()


class Gather:
    def __init__(self, copies, c, axis, own, dst, half):
        self.copies, self.c, self.axis, self.own, self.dst, self.half = copies, c, axis, own, dst, half

    def first(self):
        a = self.c[self.axis]
        self.right, self.left = peer(self.c, self.axis, 1), peer(self.c, self.axis, 3)
        self.go_right = self.copies.remote(self.own, self.dst(a), self.right)
        self.go_left = self.copies.remote(self.own, self.dst(a), self.left)

    def second(self):
        a = self.c[self.axis]
        before, after = lax.rem(a + 3, 4), lax.rem(a + 1, 4)
        self.go_right.wait_recv()
        self.on_right = self.copies.remote(self.half(before, 0), self.half(before, 0), self.right)
        self.go_left.wait_recv()
        self.on_left = self.copies.remote(self.half(after, 1), self.half(after, 1), self.left)

    def third(self):
        self.on_right.wait_recv()
        self.on_left.wait_recv()


def run_gathers(gathers):
    for g in gathers:
        g.first()
    for g in gathers:
        g.second()


def comm_call(body, live, axes, steps, count, ins, out_shapes, collective_id, aliases=None):
    n_in, n_out = len(ins), len(out_shapes)

    def kernel(*refs):
        in_refs, out_refs = refs[:n_in], refs[n_in : n_in + n_out]
        send, recv = refs[n_in + n_out :]

        def act():
            c = coords()
            meet(c, axes, steps)
            body(Copies(send, recv), c, in_refs, out_refs)

        if live is None:
            act()
        else:
            pl.when(lax.axis_index("section") == live)(act)

    return pl.pallas_call(
        kernel,
        out_shape=tuple(out_shapes),
        in_specs=[pl.BlockSpec(memory_space=HBM)] * n_in,
        out_specs=tuple([pl.BlockSpec(memory_space=HBM)] * n_out),
        scratch_shapes=[pltpu.SemaphoreType.DMA((count,)), pltpu.SemaphoreType.DMA((count,))],
        input_output_aliases=aliases or {},
        compiler_params=pltpu.CompilerParams(collective_id=collective_id, has_side_effects=True),
    )(*ins)


def gather_first(qkv, out, up, down, small):
    def body(copies, c, ins, outs):
        y, x = c["y"], c["x"]
        q_in, o_in, u_in, d_in, s_in = ins
        q_y, o_y, u_y, d_x, s_x = outs
        gathers = [
            Gather(copies, c, "y", u_in, lambda i: u_y.at[i], lambda i, h: u_y.at[i, :, pl.ds(1536 * h, 1536)]),
            Gather(copies, c, "y", q_in, lambda i: q_y.at[i], lambda i, h: q_y.at[i, pl.ds(2 * h, 2)]),
            Gather(copies, c, "y", o_in, lambda i: o_y.at[i], lambda i, h: o_y.at[i, :, pl.ds(384 * h, 384)]),
            Gather(copies, c, "x", d_in, lambda i: d_x.at[i], lambda i, h: d_x.at[i, :, pl.ds(384 * h, 384)]),
            Gather(copies, c, "x", s_in, lambda i: s_x.at[i], lambda i, h: s_x.at[i, h]),
        ]
        own = [
            copies.local(u_in, u_y.at[y]),
            copies.local(q_in, q_y.at[y]),
            copies.local(o_in, o_y.at[y]),
            copies.local(d_in, d_x.at[x]),
            copies.local(s_in, s_x.at[x]),
        ]
        run_gathers(gathers)
        for g in gathers:
            g.third()
        for copy in own:
            copy.wait()
        copies.drain()

    shapes = (
        sds((4, 4, 12, 576), BF),
        sds((4, 12, D), BF),
        sds((4, 12, FF), BF),
        sds((4, 48, D), BF),
        sds((4, 2, 8, 128), F32),
    )
    return comm_call(body, None, ("x", "y"), (1, 3), 25, (qkv, out, up, down, small), shapes, 0)


def gather_rest(live, qkv, out, up, down, small, previous, collective_id):
    def body(copies, c, ins, outs):
        x, y, z = c["x"], c["y"], c["z"]
        q_in, o_in, u_in, d_in, s_in = ins[:5]
        q, o, u, d, s = outs
        one = [
            Gather(copies, c, "z", q_in, lambda i: q.at[:, i, x], lambda i, h: q.at[pl.ds(2 * h, 2), i, x]),
            Gather(copies, c, "z", o_in, lambda i: o.at[i, x], lambda i, h: o.at[i, x, :, pl.ds(384 * h, 384)]),
            Gather(copies, c, "x", u_in, lambda i: u.at[z, i], lambda i, h: u.at[z, i, :, pl.ds(1536 * h, 1536)]),
            Gather(copies, c, "z", d_in, lambda i: d.at[i, :, y], lambda i, h: d.at[i, pl.ds(2 * h, 2), y]),
            Gather(copies, c, "z", s_in, lambda i: s.at[i, :, y], lambda i, h: s.at[i, pl.ds(2 * h, 2), y]),
        ]
        own = [
            copies.local(q_in, q.at[:, z, x]),
            copies.local(o_in, o.at[z, x]),
            copies.local(u_in, u.at[z, x]),
            copies.local(d_in, d.at[z, :, y]),
            copies.local(s_in, s.at[z, :, y]),
        ]
        run_gathers(one)
        two = [
            Gather(copies, c, "x", q.at[:, :, x], lambda i: q.at[:, :, i], lambda i, h: q.at[pl.ds(2 * h, 2), :, i]),
            Gather(copies, c, "x", o.at[:, x], lambda i: o.at[:, i], lambda i, h: o.at[pl.ds(2 * h, 2), i]),
            Gather(copies, c, "z", u.at[z], lambda i: u.at[i], lambda i, h: u.at[i, pl.ds(2 * h, 2)]),
            Gather(copies, c, "y", d.at[:, :, y], lambda i: d.at[:, :, i], lambda i, h: d.at[pl.ds(2 * h, 2), :, i]),
            Gather(copies, c, "y", s.at[:, :, y], lambda i: s.at[:, :, i], lambda i, h: s.at[pl.ds(2 * h, 2), :, i]),
        ]
        for k in range(5):
            one[k].third()
            own[k].wait()
            two[k].first()
        for g in two:
            g.second()
        for g in two:
            g.third()
        copies.drain()

    shapes = (
        sds((4, 4, 4, 48, 576), BF),
        sds((4, 4, 48, D), BF),
        sds((4, 4, 48, FF), BF),
        sds((4, 4, 4, 48, D), BF),
        sds((4, 4, 4, 2, 8, 128), F32),
    )
    ins = (qkv, out, up, down, small)
    aliases = None
    if previous is not None:
        ins = ins + tuple(previous)
        aliases = {5 + i: i for i in range(5)}
    return comm_call(body, live, ("x", "y", "z"), (1, 3), 45, ins, shapes, collective_id, aliases)


def to_heads(live, array, previous, collective_id):
    width = array.shape[-1]

    def body(copies, c, ins, outs):
        z = c["z"]
        moves = []
        for by in (2, 1, 3):
            to = peer(c, "z", by)
            moves.append(copies.remote(ins[0].at[to["seq"]], outs[0].at[:, z], to))
        own = copies.local(ins[0].at[z], outs[0].at[:, z])
        for move in moves:
            move.wait_recv()
        own.wait()
        copies.drain()

    ins, aliases = (array,), None
    if previous is not None:
        ins, aliases = (array, previous), {1: 0}
    return comm_call(
        body, live, ("z",), (1, 2, 3), 4, ins, (sds((4, 4, ROWS, width), BF),), collective_id, aliases
    )[0]


def to_tokens(live, array, previous, collective_id):
    width = array.shape[-1]

    def body(copies, c, ins, outs):
        z = c["z"]
        moves = []
        for by in (2, 1, 3):
            to = peer(c, "z", by)
            moves.append(copies.remote(ins[0].at[:, to["seq"]], outs[0].at[z], to))
        own = copies.local(ins[0].at[:, z], outs[0].at[z])
        for move in moves:
            move.wait_recv()
        own.wait()
        copies.drain()

    ins, aliases = (array,), None
    if previous is not None:
        ins, aliases = (array, previous), {1: 0}
    return comm_call(
        body, live, ("z",), (1, 2, 3), 4, ins, (sds((4, 4, ROWS, width), BF),), collective_id, aliases
    )[0]


def exchange(live, parts, collective_id):
    shapes = []
    for array, axis, dim in parts:
        shapes.append(sds((4,) + array.shape[:dim] + array.shape[dim + 1 :], array.dtype))
    axes = tuple(sorted({axis for _, axis, _ in parts}))

    def body(copies, c, ins, outs):
        moves, own = [], []
        for by in (2, 1, 3):
            for ref, out, (_, axis, dim) in zip(ins, outs, parts):
                to = peer(c, axis, by)
                there = lax.rem(c[axis] + by, 4)
                src = ref.at[(slice(None),) * dim + (there,)]
                moves.append(copies.remote(src, out.at[by], to))
        for ref, out, (_, axis, dim) in zip(ins, outs, parts):
            own.append(copies.local(ref.at[(slice(None),) * dim + (c[axis],)], out.at[0]))
        for move in moves:
            move.wait_recv()
        for copy in own:
            copy.wait()
        copies.drain()

    return comm_call(
        body, live, axes, (1, 2, 3), 4 * len(parts), tuple(p[0] for p in parts), shapes, collective_id
    )


def added(terms, dtype):
    return jnp.sum(terms.astype(F32), axis=0).astype(dtype)


def reduce_grads(live, qkv, out, up, down, small, base_id):
    q, o, u, d, s = exchange(
        live,
        ((qkv, "x", 2), (out, "x", 1), (up, "z", 0), (down, "y", 2), (small, "y", 2)),
        base_id,
    )
    q, o, u, d, s = added(q, BF), added(o, BF), added(u, BF), added(d, BF), added(s, F32)
    q, o, u, d, s = exchange(
        live, ((q, "z", 1), (o, "z", 0), (u, "x", 0), (d, "z", 0), (s, "z", 0)), base_id + 1
    )
    q, o, u, d, s = added(q, BF), added(o, BF), added(u, BF), added(d, BF), added(s, F32)
    q, o, u = q.reshape(4, 4, 12, 576), o.reshape(4, 12, D), u.reshape(4, 12, FF)
    return exchange(
        live, ((q, "y", 1), (o, "y", 0), (u, "y", 0), (d, "x", 0), (s, "x", 0)), base_id + 2
    )


BIG = pltpu.CompilerParams(vmem_limit_bytes=56 * 1024 * 1024)


def dot(a, b):
    return jnp.dot(a, b, preferred_element_type=F32)


def dot_nt(a, b):
    return lax.dot_general(a, b, (((1,), (1,)), ((), ())), preferred_element_type=F32)


def dot_tn(a, b):
    return lax.dot_general(a, b, (((0,), (0,)), ((), ())), preferred_element_type=F32)


def normalize(values):
    centered = values - jnp.mean(values, axis=-1, keepdims=True)
    spread = jnp.mean(centered * centered, axis=-1, keepdims=True)
    inverse = lax.rsqrt(spread + EPSILON)
    return centered * inverse, inverse


def norm_back(e, n, inverse):
    return inverse * (
        e - jnp.mean(e, axis=-1, keepdims=True) - n * jnp.mean(e * n, axis=-1, keepdims=True)
    )


def gelu_parts(u):
    inner = 0.7978845608 * (u + 0.044715 * (u * u * u))
    t = jnp.tanh(inner)
    return t


def whole(shape):
    zeros = (0,) * len(shape)
    return pl.BlockSpec(shape, lambda j: zeros)


def project_kernel(x_ref, vec_ref, bias_ref, w_ref, out_ref, n_ref):
    @pl.when(pl.program_id(0) == 0)
    def _():
        n, _ = normalize(x_ref[...].astype(F32))
        n_ref[...] = (n * vec_ref[0:1, :] + vec_ref[2:3, :]).astype(BF)

    out_ref[0] = (dot(n_ref[...], w_ref[0]) + bias_ref[0]).astype(BF)


def project(x, vec, bias, w):
    return pl.pallas_call(
        project_kernel,
        grid=(4,),
        out_shape=sds((4, TOK, 576), BF),
        in_specs=[
            whole((TOK, D)),
            whole((16, D)),
            pl.BlockSpec((1, 1, 576), lambda j: (j, 0, 0)),
            pl.BlockSpec((1, D, 576), lambda j: (j, 0, 0)),
        ],
        out_specs=pl.BlockSpec((1, TOK, 576), lambda j: (j, 0, 0)),
        scratch_shapes=[pltpu.VMEM((TOK, D), BF)],
        compiler_params=BIG,
    )(x, vec, bias, w)


BLOCK = 256


def masked(scores, block):
    rows = block * BLOCK + lax.broadcasted_iota(jnp.int32, scores.shape, 0)
    cols = lax.broadcasted_iota(jnp.int32, scores.shape, 1)
    return jnp.where(cols <= rows, scores, MASKED)


def attend_kernel(h_ref, o_ref, lse_ref):
    for head in range(3):
        q_at, k_at, v_at = HEAD * head, HL + HEAD * head, 2 * HL + HEAD * head
        for block in range(SEQ_LEN // BLOCK):
            rows, keys = pl.ds(block * BLOCK, BLOCK), (block + 1) * BLOCK
            q = h_ref[rows, q_at : q_at + HEAD] * jnp.asarray(0.125, BF)
            scores = masked(dot_nt(q, h_ref[0:keys, k_at : k_at + HEAD]), block)
            top = jnp.max(scores, axis=-1, keepdims=True)
            e = jnp.exp(scores - top)
            total = jnp.sum(e, axis=-1, keepdims=True)
            mixed = dot(e.astype(BF), h_ref[0:keys, v_at : v_at + HEAD])
            o_ref[rows, q_at : q_at + HEAD] = (mixed / total).astype(BF)
            lse_ref[rows, head : head + 1] = top + jnp.log(total)


def attend(heads):
    return pl.pallas_call(
        attend_kernel,
        out_shape=(sds((SEQ_LEN, HL), BF), sds((SEQ_LEN, 128), F32)),
        compiler_params=BIG,
    )(heads)


def attend_back_kernel(h_ref, lse_ref, g_ref, out_ref, dk_ref, dv_ref):
    for head in range(3):
        q_at, k_at, v_at = HEAD * head, HL + HEAD * head, 2 * HL + HEAD * head
        for block in reversed(range(SEQ_LEN // BLOCK)):
            rows, keys = pl.ds(block * BLOCK, BLOCK), (block + 1) * BLOCK
            q = h_ref[rows, q_at : q_at + HEAD] * jnp.asarray(0.125, BF)
            k = h_ref[0:keys, k_at : k_at + HEAD]
            g = g_ref[rows, q_at : q_at + HEAD]
            scores = masked(dot_nt(q, k), block)
            p = jnp.exp(scores - lse_ref[rows, head : head + 1])
            dp = dot_nt(g, h_ref[0:keys, v_at : v_at + HEAD])
            centre = jnp.sum(p * dp, axis=-1, keepdims=True)
            ds = (p * (dp - centre)).astype(BF)
            out_ref[rows, q_at : q_at + HEAD] = (dot(ds, k) * 0.125).astype(BF)
            dk = dot_tn(ds, q)
            dv = dot_tn(p.astype(BF), g)
            if block == SEQ_LEN // BLOCK - 1:
                dk_ref[...] = dk
                dv_ref[...] = dv
            else:
                dk_ref[0:keys, :] += dk
                dv_ref[0:keys, :] += dv
        out_ref[:, k_at : k_at + HEAD] = dk_ref[...].astype(BF)
        out_ref[:, v_at : v_at + HEAD] = dv_ref[...].astype(BF)


def attend_back(heads, lse, grads):
    return pl.pallas_call(
        attend_back_kernel,
        out_shape=sds((SEQ_LEN, 576), BF),
        scratch_shapes=[pltpu.VMEM((SEQ_LEN, HEAD), F32), pltpu.VMEM((SEQ_LEN, HEAD), F32)],
        compiler_params=BIG,
    )(heads, lse, grads)


def mlp_kernel(x_ref, m_ref, vec_ref, ub_ref, wo_ref, wu_ref, wd_ref, res_ref, mid_ref, raised_ref, n_ref, acc_ref):
    step = pl.program_id(0)

    @pl.when(step == 0)
    def _():
        branch = dot(m_ref[0], wo_ref[0])
        for p in range(1, 4):
            branch += dot(m_ref[p], wo_ref[p])
        middle = x_ref[...].astype(F32) + (branch + vec_ref[6:7, :])
        mid_ref[...] = middle
        n, _ = normalize(middle)
        n_ref[...] = (n * vec_ref[1:2, :] + vec_ref[3:4, :]).astype(BF)
        acc_ref[...] = middle + vec_ref[7:8, :]

    raised = dot(n_ref[...], wu_ref[...]) + ub_ref[0]
    raised_ref[...] = raised
    active = (0.5 * raised * (1.0 + gelu_parts(raised))).astype(BF)
    acc_ref[...] += dot(active, wd_ref[...])

    @pl.when(step == 3)
    def _():
        res_ref[...] = acc_ref[...].astype(BF)


def mlp(x, mixed, vec, ub, wo, wu, wd):
    return pl.pallas_call(
        mlp_kernel,
        grid=(4,),
        out_shape=(sds((TOK, D), BF), sds((TOK, D), F32), sds((TOK, FF), F32)),
        in_specs=[
            whole((TOK, D)),
            whole((4, TOK, HL)),
            whole((16, D)),
            pl.BlockSpec((1, 1, D), lambda j: (j, 0, 0)),
            whole((4, HL, D)),
            pl.BlockSpec((D, D), lambda j: (0, j)),
            pl.BlockSpec((D, D), lambda j: (j, 0)),
        ],
        out_specs=(whole((TOK, D)), whole((TOK, D)), pl.BlockSpec((TOK, D), lambda j: (0, j))),
        scratch_shapes=[pltpu.VMEM((TOK, D), BF), pltpu.VMEM((TOK, D), F32)],
        compiler_params=BIG,
    )(x, mixed, vec, ub, wo, wu, wd)


def mlp_back_kernel(
    g_ref, raised_ref, mid_ref, m_ref, vec_ref, wo_ref, wu_ref, wd_ref,
    gd_ref, gu_ref, go_ref, gm_ref, gmid_ref, sums_ref, gub_ref, n_ref, acc_ref,
):
    step = pl.program_id(0)

    @pl.when(step == 0)
    def _():
        n, _ = normalize(mid_ref[...])
        n_ref[...] = (n * vec_ref[1:2, :] + vec_ref[3:4, :]).astype(BF)
        acc_ref[...] = jnp.zeros_like(acc_ref)

    g = g_ref[...]
    u = raised_ref[...]
    t = gelu_parts(u)
    active = (0.5 * u * (1.0 + t)).astype(BF)
    gd_ref[...] = dot_tn(active, g).astype(BF)
    slope = 0.5 * (1.0 + t) + 0.5 * u * (1.0 - t * t) * (
        0.7978845608 * (1.0 + 3.0 * 0.044715 * (u * u))
    )
    grad_raised = (dot_nt(g, wd_ref[...]) * slope).astype(BF)
    gub_ref[0] = jnp.sum(grad_raised.astype(F32), axis=0, keepdims=True)
    gu_ref[...] = dot_tn(n_ref[...], grad_raised).astype(BF)
    acc_ref[...] += dot_nt(grad_raised, wu_ref[...])

    @pl.when(step == 3)
    def _():
        n, inverse = normalize(mid_ref[...])
        back = acc_ref[...]
        g32 = g.astype(F32)
        grad_middle = g32 + norm_back(back * vec_ref[1:2, :], n, inverse)
        gmid_ref[...] = grad_middle
        branch = grad_middle.astype(BF)
        sums_ref[...] = jnp.zeros_like(sums_ref)
        sums_ref[0:1, :] = jnp.sum(back * n, axis=0, keepdims=True)
        sums_ref[1:2, :] = jnp.sum(back, axis=0, keepdims=True)
        sums_ref[2:3, :] = jnp.sum(branch.astype(F32), axis=0, keepdims=True)
        sums_ref[3:4, :] = jnp.sum(g32, axis=0, keepdims=True)
        for p in range(4):
            go_ref[p] = dot_tn(m_ref[p], branch).astype(BF)
            gm_ref[p] = dot_nt(branch, wo_ref[p]).astype(BF)


def mlp_back(g, raised, middle, mixed, vec, wo, wu, wd):
    return pl.pallas_call(
        mlp_back_kernel,
        grid=(4,),
        out_shape=(
            sds((FF, D), BF),
            sds((D, FF), BF),
            sds((4, HL, D), BF),
            sds((4, TOK, HL), BF),
            sds((TOK, D), F32),
            sds((8, D), F32),
            sds((4, 1, D), F32),
        ),
        in_specs=[
            whole((TOK, D)),
            pl.BlockSpec((TOK, D), lambda j: (0, j)),
            whole((TOK, D)),
            whole((4, TOK, HL)),
            whole((16, D)),
            whole((4, HL, D)),
            pl.BlockSpec((D, D), lambda j: (0, j)),
            pl.BlockSpec((D, D), lambda j: (j, 0)),
        ],
        out_specs=(
            pl.BlockSpec((D, D), lambda j: (j, 0)),
            pl.BlockSpec((D, D), lambda j: (0, j)),
            whole((4, HL, D)),
            whole((4, TOK, HL)),
            whole((TOK, D)),
            whole((8, D)),
            pl.BlockSpec((1, 1, D), lambda j: (j, 0, 0)),
        ),
        scratch_shapes=[pltpu.VMEM((TOK, D), BF), pltpu.VMEM((TOK, D), F32)],
        compiler_params=BIG,
    )(g, raised, middle, mixed, vec, wo, wu, wd)


def project_back_kernel(x_ref, gp_ref, gmid_ref, vec_ref, w_ref, gw_ref, gx_ref, sums_ref, gb_ref, n_ref, acc_ref):
    step = pl.program_id(0)

    @pl.when(step == 0)
    def _():
        n, _ = normalize(x_ref[...].astype(F32))
        n_ref[...] = (n * vec_ref[0:1, :] + vec_ref[2:3, :]).astype(BF)
        acc_ref[...] = jnp.zeros_like(acc_ref)

    gp = gp_ref[0]
    gw_ref[0] = dot_tn(n_ref[...], gp).astype(BF)
    gb_ref[0] = jnp.sum(gp.astype(F32), axis=0, keepdims=True)
    acc_ref[...] += dot_nt(gp, w_ref[0])

    @pl.when(step == 3)
    def _():
        n, inverse = normalize(x_ref[...].astype(F32))
        back = acc_ref[...]
        gx_ref[...] = (gmid_ref[...] + norm_back(back * vec_ref[0:1, :], n, inverse)).astype(BF)
        sums_ref[...] = jnp.zeros_like(sums_ref)
        sums_ref[0:1, :] = jnp.sum(back * n, axis=0, keepdims=True)
        sums_ref[1:2, :] = jnp.sum(back, axis=0, keepdims=True)


def project_back(x, gp, gmid, vec, w):
    return pl.pallas_call(
        project_back_kernel,
        grid=(4,),
        out_shape=(sds((4, D, 576), BF), sds((TOK, D), BF), sds((8, D), F32), sds((4, 1, 576), F32)),
        in_specs=[
            whole((TOK, D)),
            pl.BlockSpec((1, TOK, 576), lambda j: (j, 0, 0)),
            whole((TOK, D)),
            whole((16, D)),
            pl.BlockSpec((1, D, 576), lambda j: (j, 0, 0)),
        ],
        out_specs=(
            pl.BlockSpec((1, D, 576), lambda j: (j, 0, 0)),
            whole((TOK, D)),
            whole((8, D)),
            pl.BlockSpec((1, 1, 576), lambda j: (j, 0, 0)),
        ),
        scratch_shapes=[pltpu.VMEM((TOK, D), BF), pltpu.VMEM((TOK, D), F32)],
        compiler_params=BIG,
    )(x, gp, gmid, vec, w)


def unpack_small(small):
    flat = small.reshape(64, 2048)
    rows = flat[:, :96].reshape(64, 8, 12).transpose(1, 0, 2).reshape(8, D)
    up = flat[:, 96:144].reshape(4, 1, D)
    vec = jnp.concatenate([rows, jnp.zeros((8, D), F32)])
    bias = jnp.concatenate([rows[4].reshape(4, HL), jnp.zeros((4, HL), F32), rows[5].reshape(4, HL)], axis=1)
    return vec, bias.reshape(4, 1, 576), up


def open_weights(raw):
    qkv, out, up, down, small = raw
    vec, bias, ub = unpack_small(small)
    return (
        qkv.reshape(4, D, 576),
        out.reshape(4, HL, D),
        up.reshape(D, FF),
        down.reshape(FF, D),
        vec,
        bias,
        ub,
    )


def forward(live, x, weights, previous, base_id):
    qkv, wo, wu, wd, vec, bias, ub = weights
    projected = project(x, vec, bias, qkv)
    heads4 = to_heads(live, projected.reshape(4, 4, ROWS, 576), previous[0], base_id)
    heads = heads4.reshape(SEQ_LEN, 576)
    mixed_heads, lse = attend(heads)
    mixed4 = to_tokens(live, mixed_heads.reshape(4, 4, ROWS, HL), previous[1], base_id + 1)
    mixed = mixed4.reshape(4, TOK, HL)
    result, middle, raised = mlp(x, mixed, vec, ub, wo, wu, wd)
    return result, (heads, lse, mixed, middle, raised), (heads4, mixed4)


def backward(live, g, x, weights, saved, previous, base_id):
    qkv, wo, wu, wd, vec, bias, ub = weights
    heads, lse, mixed, middle, raised = saved
    g_down, g_up, g_out, g_mixed, g_middle, sums_two, g_ub = mlp_back(
        g, raised, middle, mixed, vec, wo, wu, wd
    )
    g_heads4 = to_heads(live, g_mixed.reshape(4, 4, ROWS, HL), previous[0], base_id)
    g_split = attend_back(heads, lse, g_heads4.reshape(SEQ_LEN, HL))
    g_proj4 = to_tokens(live, g_split.reshape(4, 4, ROWS, 576), previous[1], base_id + 1)
    g_qkv, g_x, sums_one, g_bias = project_back(x, g_proj4.reshape(4, TOK, 576), g_middle, vec, qkv)
    rows = jnp.concatenate(
        [
            sums_one[0:1],
            sums_two[0:1],
            sums_one[1:2],
            sums_two[1:2],
            g_bias[:, 0, :HL].reshape(1, D),
            g_bias[:, 0, 2 * HL :].reshape(1, D),
            sums_two[2:4],
        ]
    )
    small = jnp.concatenate(
        [
            rows.reshape(8, 64, 12).transpose(1, 0, 2).reshape(64, 96),
            g_ub.reshape(64, 48),
            jnp.zeros((64, 1024 - 144), F32),
        ],
        axis=1,
    )
    grads = (
        g_qkv.reshape(4, 4, 4, 48, 576),
        g_out.reshape(4, 4, 48, D),
        g_up.reshape(4, 4, 48, FF),
        g_down.reshape(4, 4, 4, 48, D),
        small.reshape(4, 4, 4, 8, 128),
    )
    return g_x, grads, (g_heads4, g_proj4)


def per_device(ends, w_qkv, w_out, w_up, w_down, norm_gains, biases, up_bias):
    section = lax.axis_index("section")
    own = ends.reshape(TOK, D)
    qkv = w_qkv[0].reshape(12, 3, 4, HL).transpose(2, 0, 1, 3).reshape(4, 12, 576)
    small = jnp.concatenate(
        [norm_gains.reshape(-1), biases.reshape(-1), up_bias.reshape(-1), jnp.zeros((2048 - 144,), BF)]
    ).astype(F32)
    q_y, o_y, u_y, d_x, s_x = gather_first(qkv, w_out[0], w_up[0], w_down[0], small.reshape(2, 8, 128))
    first = (
        q_y.transpose(1, 0, 2, 3).reshape(4, 48, 576),
        o_y.reshape(48, D),
        u_y.reshape(48, FF),
        d_x,
        s_x,
    )
    raw = gather_rest(0, *first, None, 1)
    result, _, kept = forward(0, own, open_weights(raw), (None, None), 3)
    arriving = lax.ppermute(result, "section", [(0, 1)])
    raw, arriving = lax.optimization_barrier((raw, arriving))
    raw = gather_rest(1, *first, raw, 2)
    weights = open_weights(raw)
    x = jnp.where(section == 0, own, arriving)
    result, saved, _ = forward(1, x, weights, kept, 5)

    g_x, grads, _ = backward(1, own, x, weights, saved, (None, None), 7)
    arriving = lax.ppermute(g_x, "section", [(1, 0)])
    grads, arriving = lax.optimization_barrier((grads, arriving))
    total_one = reduce_grads(1, *grads, 11)
    total_one, arriving = lax.optimization_barrier((total_one, arriving))
    g = jnp.where(section == 1, own, arriving)
    g_x, grads, _ = backward(0, g, x, weights, saved, (None, None), 9)
    total_zero = reduce_grads(0, *grads, 14)
    q, o, u, d, s = (
        added(jnp.where(section == 0, zero, one), F32) for zero, one in zip(total_zero, total_one)
    )
    flat = s.reshape(1024)
    boundary = jnp.where(section == 0, g_x, result)
    return (
        boundary.reshape(1, 1, GROUPS, ROWS, D),
        q.reshape(4, 12, 3, HL).transpose(1, 2, 0, 3).reshape(1, 12, 3 * D),
        o[None],
        u[None],
        d[None],
        flat[:24].reshape(1, 2, 12),
        flat[24:96].reshape(1, 6, 12),
        flat[96:144].reshape(1, 48),
    )


def solution(mesh):
    rows = P("section", ("seq", "shard"), None)
    columns = P("section", None, ("seq", "shard"))
    ends = P("section", "shard", None, "seq", None)
    hidden = P("section", ("seq", "shard"))
    placed = (ends, rows, rows, rows, rows, columns, columns, hidden)
    return jax.shard_map(per_device, mesh=mesh, in_specs=placed, out_specs=placed, check_vma=False)
```

time: 2380 us -> 580 us (0.24)
  blocking collectives: 1140 us -> 0 us
  Pallas kernels: 0 us -> 395 us
  local copies, waits for them, and re-layouts: 364 us -> 36.3 us
  matrix products: 311 us -> 0 us
  starting transfers between devices: 279 us -> 2.59 us
  other arithmetic: 152 us -> 42.1 us
    unnamed x3 -> x0, blocking collectives: 797 us -> none
    pallas_call x0 -> x29, Pallas kernels: none -> 395 us  [the longest x17 279 us: comm_call(): pl.pallas_call(kernel, out_shape=tuple(out_shapes), in_specs=[pl.BlockSpe...]
    all_gather x2 -> x0, blocking collectives: 346 us -> none  [the longest x1 173 us: gather_weights(): lax.all_gather(shard_gains, ('seq', 'shard'), axis=2, tiled=True)]
    dot_general x95 -> x0, matrix products: 311 us -> none  [the longest x5 40.8 us: backward_group(): jnp.dot(normed_two.astype(jnp.bfloat16).T, grad_raised, preferred_element...]
    unnamed x48 -> x0, starting transfers between devices: 180 us -> none
    unnamed x405 -> x56, local copies, waits for them, and re-layouts: 126 us -> 1.61 us
    ppermute x8 -> x2, waiting for transfers between devices: 0.02 us -> 92.2 us  [the longest x1 90.7 us: per_device(): arriving = lax.ppermute(g_x, 'section', [(1, 0)])]
    all_to_all x20 -> x0, waiting for transfers between devices: 88.9 us -> none  [the longest x5 42.8 us: backward_group(): lax.all_to_all(grad_split.reshape(group_rows, 3, 1, width // parts), 'seq...]
  transfers between devices with their start and end apart: 81 -> 2, of which waited for: 17 -> 2; matrix products, arithmetic and copies ran while one was open for 26% -> 1% of each run, Pallas kernels for 0% -> 0%
where the time goes in v1:
time: 580 us; the launch traced here: 570 us
  Pallas kernels  395 us (68%)
  waiting for transfers between devices  92.2 us (16%)
  other arithmetic  42.1 us (7%)
  local copies, waits for them, and re-layouts  36.3 us (6%)
    pallas_call x17, Pallas kernels, comm_call(): pl.pallas_call(kernel, out_shape=tuple(out_shapes), in_specs=[pl.BlockSpe...  279 us
    ppermute x1, waiting for transfers between devices, per_device(): arriving = lax.ppermute(g_x, 'section', [(1, 0)])  90.7 us
    reduce_sum x25, other arithmetic, added(): return jnp.sum(terms.astype(F32), axis=0).astype(dtype)  38.8 us
    pallas_call x2, Pallas kernels, mlp_back(): pl.pallas_call(mlp_back_kernel, grid=(4,), out_shape=(sds((FF, D), BF), s...  31.5 us
    pallas_call x2, Pallas kernels, attend_back(): pl.pallas_call(attend_back_kernel, out_shape=sds((SEQ_LEN, 576), BF), scr...  23.4 us
    pallas_call x2, Pallas kernels, mlp(): pl.pallas_call(mlp_kernel, grid=(4,), out_shape=(sds((TOK, D), BF), sds((...  19.5 us
    pallas_call x2, Pallas kernels, project_back(): pl.pallas_call(project_back_kernel, grid=(4,), out_shape=(sds((4, D, 576)...  15.9 us
    pallas_call x2, Pallas kernels, attend(): pl.pallas_call(attend_kernel, out_shape=(sds((SEQ_LEN, HL), BF), sds((SEQ...  14.9 us
  transfers between devices with their start and end apart: 2, of which 2 were waited for; matrix products, arithmetic and copies ran while one was open for 1% of the time, Pallas kernels for 0%

profile of v1, /device:TPU:2, one launch (start us, length us, event | category | flops | bytes accessed | tf_op | source)
XLA Modules:
  0.0 569.8 jit_solution(6718290562645513678)
XLA Ops:
  3.5 1.0 reshape_squeeze.19
  5.3 14.8 %shard_map.143 = (bf16[4,4,12,576]{3,2,1,0:T(8,128)(2,1)}, bf16[4,12,768]{2,1,0:T(8,128)(2,1)}, bf16[4,12,3072]{2,1,0:T(8,128)(2,1)}, bf16[4,48,768]{2,1,0:T(8,128)(2,1)}, f32[4,2,8,128]{3,2,1,0:T(8,128)}) custom-call(bf16[4,12,576]{2,1,0:T(8,128)(2,1)} %copy.78.refs_0_, bf16[12,768]{1,0:T(8,128)(2,1)} %bitcast.150, bf16[12,3072]{1,0:T(8,128)(2,1)} %bitcast.148, ...), custom_call_target="tpu_custom_call" | custom-call | tf_op jit(solution)/shard_map/pallas_call | solution.py:125
  20.2 1.1 copy.79
  22.0 1.5 reshape.261.refs_1_
  24.4 59.0 %shard_map.144 = (bf16[4,4,4,48,576]{4,3,2,1,0:T(8,128)(2,1)}, bf16[4,4,48,768]{3,2,1,0:T(8,128)(2,1)}, bf16[4,4,48,3072]{3,2,1,0:T(8,128)(2,1)}, bf16[4,4,4,48,...) custom-call(bf16[4,48,576]{2,1,0:T(8,128)(2,1)} %copy.80.refs_0_, bf16[48,768]{1,0:T(8,128)(2,1)} %reshape.261.refs_1_, ...), custom_call_target="tpu_custom_call" | custom-call | tf_op jit(solution)/shard_map/pallas_call | solution.py:125
  83.4 1.1 reshape.263
  87.4 5.3 shard_map.145
  92.8 12.6 %shard_map.146.refs_1_ = bf16[4,4,64,576]{3,2,1,0:T(8,128)(2,1)} custom-call(bf16[4,4,64,576]{3,2,1,0:T(8,128)(2,1)} %bitcast.116), custom_call_target="tpu_custom_call" | custom-call | tf_op jit(solution)/shard_map/pallas_call | solution.py:125
  105.3 7.4 %shard_map.147 = (bf16[1024,192]{1,0:T(8,128)(2,1)}, f32[1024,128]{1,0:T(8,128)}) custom-call(bf16[1024,576]{1,0:T(8,128)(2,1)} %bitcast.97), custom_call_target="tpu_custom_call" | custom-call | tf_op jit(solution)/shard_map/pallas_call | solution.py:408
  112.8 8.1 %shard_map.148.refs_1_ = bf16[4,4,64,192]{3,2,1,0:T(8,128)(2,1)} custom-call(bf16[4,4,64,192]{3,2,1,0:T(8,128)(2,1)} %bitcast.137), custom_call_target="tpu_custom_call" | custom-call | tf_op jit(solution)/shard_map/pallas_call | solution.py:125
  120.9 9.8 %shard_map.149 = (bf16[256,768]{1,0:T(8,128)(2,1)}, f32[256,768]{1,0:T(8,128)}, f32[256,3072]{1,0:T(8,128)}) custom-call(bf16[256,768]{1,0:T(8,128)(2,1)} %bitcast.110, bf16[4,256,192]{2,1,0:T(8,128)(2,1)} %bitcast.105, f32[16,768]{1,0:T(8,128)} %concatenate.58.vec_ref, f32[4,1,768]{2,1,0:T(1,128)} %reshape.325.ub_ref, bf16[4,192,768]{2,1,0:T(8,128)(2,1)} %bitcast.101, ...), custom_call_target="tpu_custom_call" | custom-call | tf_op jit(solution)/shard_map/pallas_call | solution.py:475
  130.6 1.3 collective-permute-start
  132.0 1.4 collective-permute-done
  133.5 1.0 shard_map.150
  134.5 1.2 reshape.276
  139.3 5.3 shard_map.151
  144.7 7.4 %shard_map.153 = (bf16[1024,192]{1,0:T(8,128)(2,1)}, f32[1024,128]{1,0:T(8,128)}) custom-call(bf16[1024,576]{1,0:T(8,128)(2,1)} %bitcast.98), custom_call_target="tpu_custom_call" | custom-call | tf_op jit(solution)/shard_map/pallas_call | solution.py:408
  152.2 9.8 %shard_map.155 = (bf16[256,768]{1,0:T(8,128)(2,1)}, f32[256,768]{1,0:T(8,128)}, f32[256,3072]{1,0:T(8,128)}) custom-call(bf16[256,768]{1,0:T(8,128)(2,1)} %broadcast_select_fusion.2.x_ref, bf16[4,256,192]{2,1,0:T(8,128)(2,1)} %bitcast.106, f32[16,768]{1,0:T(8,128)} %concatenate.60.vec_ref, f32[4,1,768]{2,1,0:T(1,128)} %reshape.326.ub_ref, ...), custom_call_target="tpu_custom_call" | custom-call | tf_op jit(solution)/shard_map/pallas_call | solution.py:475
  162.0 15.7 %shard_map.156 = (bf16[3072,768]{1,0:T(8,128)(2,1)}, bf16[768,3072]{1,0:T(8,128)(2,1)}, bf16[4,192,768]{2,1,0:T(8,128)(2,1)}, bf16[4,256,192]{2,1,0:T(8,128)(2,1...) custom-call(bf16[256,768]{1,0:T(8,128)(2,1)} %bitcast.111, ...), custom_call_target="tpu_custom_call" | custom-call | tf_op jit(solution)/shard_map/pallas_call | solution.py:538
  178.3 0.8 slice_reduce_fusion.8
  179.1 11.7 %shard_map.158 = bf16[1024,576]{1,0:T(8,128)(2,1)} custom-call(bf16[1024,576]{1,0:T(8,128)(2,1)} %bitcast.99, f32[1024,128]{1,0:T(8,128)} %get-tuple-element.120.lse_ref, bf16[1024,192]{1,0:T(8,128)(2,1)} %bitcast.124), custom_call_target="tpu_custom_call" | custom-call | tf_op jit(solution)/shard_map/pallas_call | solution.py:442
  190.9 7.9 %shard_map.160 = (bf16[4,768,576]{2,1,0:T(8,128)(2,1)}, bf16[256,768]{1,0:T(8,128)(2,1)}, f32[8,768]{1,0:T(8,128)}, f32[4,1,576]{2,1,0:T(1,128)}) custom-call(bf16[256,768]{1,0:T(8,128)(2,1)} %broadcast_select_fusion.2.x_ref, bf16[4,256,576]{2,1,0:T(8,128)(2,1)} %bitcast.115, f32[256,768]{1,0:T(8,128)} %get-tuple-element.128.gmid_ref, ...), custom_call_target="tpu_custom_call" | custom-call | tf_op jit(solution)/shard_map/pallas_call | solution.py:599
  198.8 1.3 collective-permute-start.1
  202.5 0.8 slice_reduce_fusion.9
  204.9 90.7 %collective-permute-done.1 = bf16[256,768]{1,0:T(8,128)(2,1)S(1)} collective-permute-done((bf16[256,768]{1,0:T(8,128)(2,1)}, bf16[256,768]{1,0:T(8,128)(2,1)S(1)}, u32[]{:S(2)}, u32[]{:S(2)}) %collective-permute-start.1) | collective-permute-done | bytes 393248 | tf_op jit(solution)/shard_map/ppermute | solution.py:720
  296.2 4.1 reduce_sum.273.refs_0_
  300.9 0.9 reduce_sum.274.refs_1_
  301.8 4.6 reduce_sum.275.refs_2_
  306.4 4.4 reduce_sum.276.refs_3_
  311.2 1.5 reduce_sum.278
  316.0 0.9 reduce_sum.281.refs_3_
  318.1 15.8 %shard_map.164 = (bf16[3072,768]{1,0:T(8,128)(2,1)}, bf16[768,3072]{1,0:T(8,128)(2,1)}, bf16[4,192,768]{2,1,0:T(8,128)(2,1)}, bf16[4,256,192]{2,1,0:T(8,128)(2,1...) custom-call(bf16[256,768]{1,0:T(8,128)(2,1)} %broadcast_select_fusion.g_ref, ...), custom_call_target="tpu_custom_call" | custom-call | tf_op jit(solution)/shard_map/pallas_call | solution.py:538
  335.5 8.6 %shard_map.165 = bf16[4,4,64,192]{3,2,1,0:T(8,128)(2,1)} custom-call(bf16[4,4,64,192]{3,2,1,0:T(8,128)(2,1)} %bitcast.135), custom_call_target="tpu_custom_call" | custom-call | tf_op jit(solution)/shard_map/pallas_call | solution.py:125
  344.1 11.7 %shard_map.166 = bf16[1024,576]{1,0:T(8,128)(2,1)} custom-call(bf16[1024,576]{1,0:T(8,128)(2,1)} %bitcast.100, f32[1024,128]{1,0:T(8,128)} %get-tuple-element.120.lse_ref, bf16[1024,192]{1,0:T(8,128)(2,1)} %bitcast.125), custom_call_target="tpu_custom_call" | custom-call | tf_op jit(solution)/shard_map/pallas_call | solution.py:442
  355.8 12.7 %shard_map.167 = bf16[4,4,64,576]{3,2,1,0:T(8,128)(2,1)} custom-call(bf16[4,4,64,576]{3,2,1,0:T(8,128)(2,1)} %bitcast.112), custom_call_target="tpu_custom_call" | custom-call | tf_op jit(solution)/shard_map/pallas_call | solution.py:125
  368.6 8.0 %shard_map.168 = (bf16[4,768,576]{2,1,0:T(8,128)(2,1)}, bf16[256,768]{1,0:T(8,128)(2,1)}, f32[8,768]{1,0:T(8,128)}, f32[4,1,576]{2,1,0:T(1,128)}) custom-call(bf16[256,768]{1,0:T(8,128)(2,1)} %broadcast_select_fusion.2.x_ref, bf16[4,256,576]{2,1,0:T(8,128)(2,1)} %bitcast.114, f32[256,768]{1,0:T(8,128)} %get-tuple-element.161.gmid_ref, ...), custom_call_target="tpu_custom_call" | custom-call | tf_op jit(solution)/shard_map/pallas_call | solution.py:599
  376.6 0.8 slice_reduce_fusion.5
  380.6 116.7 %shard_map.169 = (bf16[4,4,4,48,576]{4,3,2,1,0:T(8,128)(2,1)}, bf16[4,4,48,768]{3,2,1,0:T(8,128)(2,1)}, bf16[4,4,48,3072]{3,2,1,0:T(8,128)(2,1)}, bf16[4,4,4,48,...) custom-call(bf16[4,4,4,48,576]{4,3,2,1,0:T(8,128)(2,1)} %bitcast.123, bf16[4,4,48,768]{3,2,1,0:T(8,128)(2,1)} %bitcast.126, ...), custom_call_target="tpu_custom_call" | custom-call | tf_op jit(solution)/shard_map/pallas_call | solution.py:125
  497.4 4.1 reduce_sum.283.refs_0_
  502.1 0.9 reduce_sum.284.refs_1_
  503.0 4.6 reduce_sum.285.refs_2_
  507.6 4.4 reduce_sum.286.refs_3_
  512.0 31.6 %shard_map.170 = (bf16[4,4,48,576]{3,2,1,0:T(8,128)(2,1)}, bf16[4,48,768]{2,1,0:T(8,128)(2,1)}, bf16[4,48,3072]{2,1,0:T(8,128)(2,1)}, bf16[4,4,48,768]{3,2,1,0:T(8,128)(2,1)}, f32[4,4,8,128]{3,2,1,0:T(8,128)}) custom-call(bf16[4,4,48,576]{3,2,1,0:T(8,128)(2,1)} %reduce_sum.283.refs_0_, bf16[4,48,768]{2,1,0:T(8,128)(2,1)} %reduce_sum.284.refs_1_, ...), custom_call_target="tpu_custom_call" | custom-call | tf_op jit(solution)/shard_map/pallas_call | solution.py:125
  543.6 1.5 reduce_sum.288
  547.6 0.9 reduce_sum.291.refs_3_
  549.4 11.8 %shard_map.171 = (bf16[4,4,12,576]{3,2,1,0:T(8,128)(2,1)}, bf16[4,12,768]{2,1,0:T(8,128)(2,1)}, bf16[4,12,3072]{2,1,0:T(8,128)(2,1)}, bf16[4,48,768]{2,1,0:T(8,128)(2,1)}, f32[4,8,128]{2,1,0:T(8,128)}) custom-call(bf16[4,4,12,576]{3,2,1,0:T(8,128)(2,1)} %copy.114.refs_0_, bf16[4,12,768]{2,1,0:T(8,128)(2,1)} %reshape.316.refs_1_, ...), custom_call_target="tpu_custom_call" | custom-call | tf_op jit(solution)/shard_map/pallas_call | solution.py:125
  562.7 1.1 convert_reduce_fusion
  567.0 0.9 reshape.327
  (187 shorter events, 37.0 us)
Async XLA Ops:
  20.2 3.4 copy-start.11
  130.6 2.8 collective-permute-start
  134.5 4.0 copy-start
  190.9 10.7 %copy-start.26 = (f32[4,1,768]{2,1,0:T(1,128)S(1)}, f32[4,1,768]{2,1,0:T(1,128)}, u32[]{:S(2)}) copy-start(f32[4,1,768]{2,1,0:T(1,128)} %get-tuple-element.136) | copy-start | bytes 36868
  198.8 96.8 %collective-permute-start.1 = (bf16[256,768]{1,0:T(8,128)(2,1)}, bf16[256,768]{1,0:T(8,128)(2,1)S(1)}, u32[]{:S(2)}, u32[]{:S(2)}) collective-permute-start(bf16[256,768]{1,0:T(8,128)(2,1)} %get-tuple-element.137), channel_id=1, source_target_pairs={{64,0},{65,1},{66,2},{67,3},{68,4},{69,5},{70,6},{71,7},{72,8},{73... | collective-permute-start | bytes 1179656 | tf_op jit(solution)/shard_map/ppermute | solution.py:720
  296.2 4.1 copy-start.18
  296.2 4.7 copy-start.6
  311.2 1.7 copy-start.23
  311.2 2.3 copy-start.17
  311.2 3.7 copy-start.5
  314.2 1.8 copy-start.2
  316.0 1.3 copy-start.1
  368.6 9.6 %copy-start.25 = (f32[4,1,768]{2,1,0:T(1,128)S(1)}, f32[4,1,768]{2,1,0:T(1,128)}, u32[]{:S(2)}) copy-start(f32[4,1,768]{2,1,0:T(1,128)} %get-tuple-element.171) | copy-start | bytes 36868
  497.3 4.1 copy-start.19
  497.3 4.7 copy-start.7
  543.6 1.7 copy-start.22
  543.6 2.3 copy-start.16
  543.6 3.7 copy-start.4
  545.9 1.7 copy-start.3
  547.6 13.7 %copy-start.24 = (f32[4,8,128]{2,1,0:T(8,128)S(1)}, f32[4,8,128]{2,1,0:T(8,128)}, u32[]{:S(2)}) copy-start(f32[4,8,128]{2,1,0:T(8,128)} %get-tuple-element.191) | copy-start | bytes 49156
  547.6 15.1 %copy-start.8 = (bf16[4,12,3072]{2,1,0:T(8,128)(2,1)S(1)}, bf16[4,12,3072]{2,1,0:T(8,128)(2,1)}, u32[]{:S(2)}) copy-start(bf16[4,12,3072]{2,1,0:T(8,128)(2,1)} %get-tuple-element.187) | copy-start | bytes 884740
  549.4 15.3 %copy-start.12 = (bf16[4,4,12,576]{3,2,1,0:T(8,128)(2,1)S(1)}, bf16[4,4,12,576]{3,2,1,0:T(8,128)(2,1)}, u32[]{:S(2)}) copy-start(bf16[4,4,12,576]{3,2,1,0:T(8,128)(2,1)} %get-tuple-element.183) | copy-start | bytes 663556
  561.2 3.4 copy-start.13
  561.2 3.6 copy-start.20
  561.2 3.6 copy-start.21
  563.8 4.0 copy-start.9
  563.9 4.0 copy-start.10
  564.7 3.9 copy-start.14
  564.7 3.9 copy-start.15
